TPU v7x, 512 devices: a whole 4x4x16 slice. The times are simulated.
512 devices in a mesh: px: 64 (over z, x), pz: 8 (over y, core).
Axes of the slice: x: 4, y: 4, z: 16, core: 2. Of those that a mesh axis runs over, the one named last changes fastest.
Arguments:
- velocity: float32 [3, 512, 512, 128], P(None, 'pz', 'px'), may hold values from -6 to 6
- metric_first: float32 [512], replicated, may hold values from 0.5 to 2
- metric_second: float32 [512], replicated, may hold values from -4 to 4
Outputs:
- tendency: float32 [3, 512, 512, 128], P(None, 'pz', 'px')
All inputs are finite; a program needn't handle non-finite values.
Results may differ from a plain program's by a relative error of at most 0.0003.
Values sent between devices are 32-bit elements; how exact they have to be, the bound alone decides.
No kernel may reach another device: no remote copies, remote signals or barrier semaphores. Data moves between devices by JAX's collectives and lax.ppermute only.
A program may use at most 64 MiB of HBM per device.

v0:
```python
import functools
import math

import jax
import jax.numpy as jnp
import numpy as np
from jax import lax
from jax.experimental import pallas as pl
from jax.experimental.pallas import tpu as pltpu
from jax.sharding import PartitionSpec as P


FIRST_ALPHA = 0.4998
FIRST_NEAR = 2.0 * (FIRST_ALPHA + 2.0) / 3.0
FIRST_FAR = (4.0 * FIRST_ALPHA - 1.0) / 3.0
SECOND_ALPHA = 2.0 / 11.0
SECOND_NEAR = 12.0 / 11.0
SECOND_FAR = 3.0 / 11.0
VISCOSITY = 0.5

COMPS = 3
YB = 64
XB = 8
LANES = 128
ROWS = COMPS * YB
GROUP = 8
PART = ROWS // GROUP
YROWS = COMPS * XB


class Line:
    def __init__(self, alpha, stencil, sign):
        root = math.sqrt(1.0 - 4.0 * alpha * alpha)
        self.r = -2.0 * alpha / (1.0 + root)
        green = [self.r ** abs(n) / root for n in range(-4, 5)]
        reply = [sum(stencil[k + 2] * green[n + k + 4] for k in range(-2, 3)) for n in (0, 1, 2)]
        self.sign = sign
        self.mid = reply[0]
        self.up = reply[2] / self.r**2
        self.near = reply[1] - self.up * self.r


ONE = Line(
    FIRST_ALPHA,
    [-FIRST_FAR / 4, -FIRST_NEAR / 2, 0.0, FIRST_NEAR / 2, FIRST_FAR / 4],
    -1.0,
)
TWO = Line(
    SECOND_ALPHA,
    [
        SECOND_FAR / 4,
        SECOND_NEAR,
        -2.0 * SECOND_NEAR - SECOND_FAR / 2,
        SECOND_NEAR,
        SECOND_FAR / 4,
    ],
    1.0,
)
LINES = (ONE, TWO)


def ring_table(groups, cells):
    pairs = groups // 2
    table = np.zeros((groups, 4 * pairs + 16))
    for q in range(groups):
        for s, line in enumerate(LINES):
            sigma = line.r**cells
            for d in range(1, pairs + 1):
                weight = sigma ** (2 * d - 2) / (1.0 - sigma**groups)
                table[q, (2 * s) * pairs + (q // 2 - d) % pairs] += weight
                table[q, (2 * s + 1) * pairs + (q // 2 + d) % pairs] += weight
            up, down = ((1.0, sigma), (sigma, 1.0)) if q % 2 else ((sigma, 1.0), (1.0, sigma))
            low, high = ((1.0, sigma), (0.0, 1.0)) if q % 2 else ((0.0, 1.0), (1.0, sigma))
            table[q, 4 * pairs + 8 * s : 4 * pairs + 8 * s + 8] = (*up, *down, *low, *high)
    return table.astype(np.float32)


def wall_table(blocks, cells):
    stages = blocks.bit_length() - 1
    table = np.zeros((blocks, 18 * stages + 12))
    for k in range(blocks):
        for stage in range(stages):
            size = 1 << stage
            inside = k % size
            below = (k >> stage) & 1
            row = table[k, 18 * stage : 18 * stage + 18]
            for s, line in enumerate(LINES):
                rho = line.r**cells
                own, other = (1.0, rho**size) if below else (rho**size, 1.0)
                row[2 * s : 2 * s + 2] = own, other
                row[6 + 2 * s : 8 + 2 * s] = other, own
                row[12 + 2 * s] = rho**inside if below else 0.0
                row[13 + 2 * s] = 0.0 if below else rho ** (size - 1 - inside)
            row[4:6] = (1.0, 0.0) if below else (0.0, 1.0)
            row[10:12] = (0.0, 1.0) if below else (1.0, 0.0)
            row[16] = float(below and inside == 0)
            row[17] = float(not below and inside == size - 1)
        row = table[k, 18 * stages :]
        for s, line in enumerate(LINES):
            rho = line.r**cells
            eps = line.r ** (blocks * cells + 1)
            up, down = line.up, line.sign * line.up
            scale = -line.r / (1.0 - eps * eps)
            low, high = rho**k / up, rho ** (blocks - 1 - k) / down
            row[4 * s : 4 * s + 4] = (
                -scale * eps * up * low,
                scale * down * low,
                scale * up * high,
                -scale * eps * down * high,
            )
            edge = line.near / (line.up * line.r)
            row[8 + s] = edge if k == 0 else 0.0
            row[10 + s] = edge if k == blocks - 1 else 0.0
    return table.astype(np.float32)


class Chosen:
    def __init__(self, table, index):
        self.table = table
        self.here = [index == j for j in range(1, len(table))]

    def __getitem__(self, m):
        value = float(self.table[0, m])
        for here, entry in zip(self.here, self.table[1:, m]):
            value = jnp.where(here, float(entry), value)
        return value


def plane(base, index):
    return pl.ds(base + index, 8, stride=XB)


def top_half(shape):
    return lax.broadcasted_iota(jnp.int32, shape, 0) % 8 < 4


def by_line(rows, one, two):
    return jnp.where(top_half((rows, LANES)), one, two)


def moments_x(v_hbm, out_hbm, v_ref, out_ref, in_sems, out_sems):
    def fetch(part):
        rows = pl.ds(part * PART * XB, PART * XB)
        return pltpu.make_async_copy(v_hbm.at[rows], v_ref.at[rows], in_sems.at[part])

    def send(part):
        return pltpu.make_async_copy(out_ref.at[part], out_hbm.at[part], out_sems.at[part])

    for part in range(GROUP):
        fetch(part).start()
    for part in range(GROUP):
        fetch(part).wait()
        for g in range(part * PART // 8, (part + 1) * PART // 8):
            sums = [None] * 4
            for i in range(XB):
                f = v_ref[plane(64 * g, i), :]
                for s, line in enumerate(LINES):
                    sums[2 * s] = f if i == 0 else sums[2 * s] * line.r + f
                    sums[2 * s + 1] = f if i == 0 else sums[2 * s + 1] + line.r**i * f
            for side in range(2):
                one, two = sums[side], sums[2 + side]
                tiles = (by_line(8, one, pltpu.roll(two, 4, 0)), by_line(8, pltpu.roll(one, 4, 0), two))
                for half in range(2):
                    at = 2 * PART * side + 2 * (8 * g + 4 * half - part * PART)
                    out_ref[part, at : at + 8, :] = tiles[half]
        send(part).start()
    for part in range(GROUP):
        send(part).wait()


def moments_y(place_ref, table_ref, v_ref, here_ref, low_ref, high_ref):
    k = place_ref[1]
    base = table_ref.shape[1] - 4
    for c in range(COMPS):
        sums = [None] * 4
        first = v_ref[c * YB * XB : c * YB * XB + XB, :]
        for y in range(YB):
            f = v_ref[(c * YB + y) * XB : (c * YB + y + 1) * XB, :]
            for s, line in enumerate(LINES):
                sums[2 * s] = f if y == 0 else sums[2 * s] * line.r + f
                sums[2 * s + 1] = f if y == 0 else sums[2 * s + 1] + line.r**y * f
        last = f
        for s in range(2):
            sums[2 * s] = sums[2 * s] + table_ref[k, base + 2 + s] * last
            sums[2 * s + 1] = sums[2 * s + 1] + table_ref[k, base + s] * first
        for m, value in enumerate((*sums, last, first)):
            here_ref[m * YROWS + c * XB : m * YROWS + (c + 1) * XB, :] = value
    for g in range(ROWS // 8):
        low_ref[8 * g : 8 * g + 8, :] = v_ref[plane(64 * g, 0), :]
        high_ref[8 * g : 8 * g + 8, :] = v_ref[plane(64 * g, XB - 1), :]


def values(ref, m):
    return ref[m * YROWS : (m + 1) * YROWS, :]


def entered(stage, weights, sibling_ref, so_far):
    terms = [weights[18 * stage + 12 + m] * values(sibling_ref, m) for m in range(6)]
    return terms if so_far is None else [value + term for value, term in zip(so_far, terms)]


def joined(stage, weights, cube_ref, sibling_ref):
    at = 18 * stage
    return [
        weights[at + m] * values(cube_ref, m) + weights[at + 6 + m] * values(sibling_ref, m) for m in range(6)
    ]


def join(stage, table, cube_ref, sibling_ref, *refs):
    weights = Chosen(table, lax.axis_index("pz"))
    *before, cube_out, entering_out = refs
    so_far = [values(before[0], m) for m in range(6)] if before else None
    for m, value in enumerate(joined(stage, weights, cube_ref, sibling_ref)):
        cube_out[m * YROWS : (m + 1) * YROWS, :] = value
    for m, value in enumerate(entered(stage, weights, sibling_ref, so_far)):
        entering_out[m * YROWS : (m + 1) * YROWS, :] = value


def group_moments(near_ref, out_ref):
    rho = by_line(2 * PART, ONE.r**XB, TWO.r**XB)
    up = near_ref[0, 0 : 2 * PART, :]
    down = near_ref[GROUP - 1, 2 * PART : 4 * PART, :]
    for j in range(1, GROUP):
        up = up * rho + near_ref[j, 0 : 2 * PART, :]
        down = down * rho + near_ref[GROUP - 1 - j, 2 * PART : 4 * PART, :]
    out_ref[0 : 2 * PART, :] = up
    out_ref[2 * PART : 4 * PART, :] = down


def pair_weight(weights, m):
    at = weights.table.shape[1] - 16 + m
    return by_line(2 * PART, weights[at], weights[at + 8])


def pair_moments(table, own_ref, sibling_ref, out_hbm, out_ref, sems):
    weights = Chosen(table, lax.axis_index("px") // GROUP)
    for side in range(2):
        rows = slice(2 * PART * side, 2 * PART * (side + 1))
        total = pair_weight(weights, 2 * side) * own_ref[rows, :]
        out_ref[rows, :] = total + pair_weight(weights, 2 * side + 1) * sibling_ref[rows, :]
    copies = [pltpu.make_async_copy(out_ref, out_hbm.at[j], sems.at[j]) for j in range(out_hbm.shape[0])]
    for copy in copies:
        copy.start()
    for copy in copies:
        copy.wait()


def entering(table, near_ref, sibling_ref, far_ref, out_hbm, out_ref, sems):
    weights = Chosen(table, lax.axis_index("px") // GROUP)
    pairs = far_ref.shape[0]
    rho = by_line(2 * PART, ONE.r**XB, TWO.r**XB)
    copies = [pltpu.make_async_copy(out_ref.at[j], out_hbm.at[j], sems.at[j]) for j in range(GROUP)]
    for side in range(2):
        rows = slice(2 * PART * side, 2 * PART * (side + 1))
        total = None
        for j in range(pairs):
            weight = by_line(2 * PART, weights[side * pairs + j], weights[(2 + side) * pairs + j])
            term = weight * far_ref[j, rows, :]
            total = term if total is None else total + term
        total = pair_weight(weights, 5 + 2 * side) * total
        total = total + pair_weight(weights, 4 + 2 * side) * sibling_ref[rows, :]
        for j in range(GROUP):
            here = j if side == 0 else GROUP - 1 - j
            out_ref[here, rows, :] = total
            if side == 1:
                copies[here].start()
            if j < GROUP - 1:
                total = total * rho + near_ref[here, rows, :]
    for copy in copies:
        copy.wait()


def local_terms(
    last, place_ref, table_ref, first_ref, second_ref, v_ref, low_ref, high_ref, cube_ref, sibling_ref, before_ref,
    acc_ref, u_ref, run_ref, y_ref,
):
    k = place_ref[1]
    so_far = [values(before_ref, m) for m in range(6)]
    weights = [table_ref[k, m] for m in range(table_ref.shape[1])]
    whole = joined(last, weights, cube_ref, sibling_ref)
    *starts, rows_below, rows_above = entered(last, weights, sibling_ref, so_far)
    for s in range(2):
        for side in range(2):
            for sign in range(2):
                weight = table_ref[k, 18 * (last + 1) + 4 * s + 2 * side + sign]
                starts[2 * s + side] = starts[2 * s + side] + weight * whole[2 * s + sign]

    def pick(total):
        return tuple(total[c * XB : (c + 1) * XB] for c in range(COMPS))

    def at(c, y):
        return pl.ds(pl.multiple_of((c * YB + y) * XB, XB), XB)

    def up(y, carry):
        ones, twos = carry
        new_one, new_two = [], []
        for c in range(COMPS):
            run_ref[0, at(c, y), :] = ones[c]
            run_ref[1, at(c, y), :] = twos[c]
            f = v_ref[at(c, y), :]
            new_one.append(ones[c] * ONE.r + f)
            new_two.append(twos[c] * TWO.r + f)
        return (tuple(new_one), tuple(new_two))

    lax.fori_loop(0, YB, up, (pick(starts[0]), pick(starts[2])), unroll=8)

    below = pick(rows_below)

    def down(step, carry):
        ones, twos, after, here = carry
        y = YB - 1 - step
        slope = first_ref[k * YB + y]
        curve = VISCOSITY * second_ref[k * YB + y]
        bend = VISCOSITY * slope * slope
        factor = curve - slope * here[1]
        new_one, new_two, before_all = [], [], []
        for c in range(COMPS):
            f = here[c]
            prior = jnp.maximum(y - 1, 0)
            before = jnp.where(y > 0, v_ref[at(c, prior), :], below[c])
            run_one = run_ref[0, at(c, y), :]
            run_two = run_ref[1, at(c, y), :]
            eta_one = (ONE.up * ONE.r) * (run_one - ones[c]) + ONE.near * (before - after[c])
            eta_two = (TWO.up * TWO.r) * (run_two + twos[c]) + TWO.near * (before + after[c]) + TWO.mid * f
            y_ref[at(c, y), :] = factor * eta_one + bend * eta_two
            new_one.append(ones[c] * ONE.r + f)
            new_two.append(twos[c] * TWO.r + f)
            before_all.append(before)
        return (tuple(new_one), tuple(new_two), here, tuple(before_all))

    top = tuple(v_ref[(c * YB + YB - 1) * XB : (c * YB + YB) * XB, :] for c in range(COMPS))
    lax.fori_loop(
        0, YB, down, (pick(starts[1]), pick(starts[3]), pick(rows_above), top), unroll=8
    )

    for g in range(ROWS // 8):
        f = [v_ref[plane(64 * g, i), :] for i in range(XB)]
        rows = slice(8 * g, 8 * g + 8)
        ext = [low_ref[rows, :]] + f + [high_ref[rows, :]]
        runs = []
        for line in LINES:
            left, right = [None], [None]
            for i in range(XB - 1):
                left.append(f[i] if i == 0 else left[-1] * line.r + f[i])
                right.append(f[XB - 1 - i] if i == 0 else right[-1] * line.r + f[XB - 1 - i])
            runs.append((left, right[::-1]))
        for i in range(XB):
            pair_one = ONE.near * (ext[i] - ext[i + 2])
            pair_two = (VISCOSITY * TWO.near) * (ext[i] + ext[i + 2]) + (VISCOSITY * TWO.mid) * f[i]
            (left, right), (left_two, right_two) = runs
            for value, sign in ((left[i], 1.0), (right[i], -1.0)):
                if value is not None:
                    pair_one = pair_one + (sign * ONE.up * ONE.r) * value
            for value in (left_two[i], right_two[i]):
                if value is not None:
                    pair_two = pair_two + (VISCOSITY * TWO.up * TWO.r) * value
            u = v_ref[plane(64 * (g % 8), i), :]
            if g < 8:
                u_ref[64 * g + 8 * i : 64 * g + 8 * i + 8, :] = u
            total = y_ref[plane(64 * g, i), :] - u * pair_one + pair_two
            acc_ref[64 * g + 8 * i : 64 * g + 8 * i + 8, :] = total


def finish(acc_ref, u_ref, far_ref, out_hbm, out_ref, sems):
    def send(part):
        rows = pl.ds(part * PART * XB, PART * XB)
        return pltpu.make_async_copy(out_ref.at[rows], out_hbm.at[rows], sems.at[part])

    for g in range(ROWS // 8):
        sums = []
        for side in range(2):
            tiles = []
            for half in range(2):
                part, at = divmod(8 * g + 4 * half, PART)
                at = 2 * PART * side + 2 * at
                tiles.append(far_ref[part, at : at + 8, :])
            sums.append(by_line(8, tiles[0], pltpu.roll(tiles[1], 4, 0)))
            sums.append(by_line(8, pltpu.roll(tiles[0], 4, 0), tiles[1]))
        left_one, left_two, right_one, right_two = sums
        for i in range(XB):
            one = (ONE.up * ONE.r ** (i + 1)) * left_one - (ONE.up * ONE.r ** (XB - i)) * right_one
            two = (VISCOSITY * TWO.up * TWO.r ** (i + 1)) * left_two
            two = two + (VISCOSITY * TWO.up * TWO.r ** (XB - i)) * right_two
            u = u_ref[64 * (g % 8) + 8 * i : 64 * (g % 8) + 8 * i + 8, :]
            acc = acc_ref[64 * g + 8 * i : 64 * g + 8 * i + 8, :]
            out_ref[plane(64 * g, i), :] = (acc + two) - u * one
        if 8 * (g + 1) % PART == 0:
            send(8 * g // PART).start()
    for part in range(GROUP):
        send(part).wait()


VMEM = pl.BlockSpec(memory_space=pltpu.VMEM)
SMEM = pl.BlockSpec(memory_space=pltpu.SMEM)
ANY = pl.BlockSpec(memory_space=pl.ANY)


def staged(shape, *counts):
    return [pltpu.VMEM(shape, jnp.float32)] + [pltpu.SemaphoreType.DMA((n,)) for n in counts]


def call(body, ins, outs, cycles, scratch=(), after=(), to=None, vmem=12):
    count = len(ins)

    def placed(*refs):
        body(*refs[:count], *refs[count + len(after) :])

    shapes = tuple(jax.ShapeDtypeStruct(s, jnp.float32) for s in outs)
    moved = 4 * sum(math.prod(s) for s in outs)
    kernel = pl.pallas_call(
        placed,
        out_shape=shapes if len(shapes) > 1 else shapes[0],
        in_specs=list(ins) + [pl.BlockSpec(memory_space=pl.ANY)] * len(after),
        out_specs=tuple(to or VMEM for _ in outs) if len(outs) > 1 else to or VMEM,
        scratch_shapes=list(scratch),
        compiler_params=pltpu.CompilerParams(vmem_limit_bytes=vmem << 20),
        cost_estimate=pl.CostEstimate(flops=cycles * 1024, bytes_accessed=2 * moved, transcendentals=0),
    )

    def run(*arrays):
        return kernel(*arrays, *after)

    return run


def on_device(velocity, metric_first, metric_second):
    px = lax.axis_size("px")
    pz = lax.axis_size("pz")
    groups = px // GROUP
    adjacent = [[GROUP * q + j for j in range(GROUP)] for q in range(groups)]
    across = [[j + 2 * GROUP * q for q in range(groups // 2)] for j in range(2 * GROUP)]
    place = jnp.stack([lax.axis_index("px") // GROUP, lax.axis_index("pz")]).astype(jnp.int32)
    ring = ring_table(groups, GROUP * XB)
    wall_rows = wall_table(pz, YB)
    wall = jnp.asarray(wall_rows)
    chunk = (GROUP, 4 * PART, LANES)
    v = velocity.reshape(ROWS * XB, LANES)

    whole = (ROWS * XB, LANES)
    scratch = [pltpu.VMEM(whole, jnp.float32)] + staged(chunk, GROUP, GROUP)
    near = call(moments_x, [ANY], [chunk], 1500, scratch, to=ANY, vmem=60)(v)
    near = lax.all_to_all(near, "px", 0, 0, tiled=True, axis_index_groups=adjacent)
    here, low, high = call(
        moments_y, [SMEM, SMEM, VMEM], [(6 * YROWS, LANES)] + [(ROWS, LANES)] * 2, 1500
    )(place, wall, v)

    def sibling_of(cube, stage):
        return lax.ppermute(cube, "pz", [(i, i ^ (1 << stage)) for i in range(pz)])

    def join_stage(stage, *arrays):
        body = functools.partial(join, stage, wall_rows)
        cube = [(6 * YROWS, LANES)] * 2
        return call(body, [VMEM] * len(arrays), cube, 200)(*arrays)

    stages = pz.bit_length() - 1
    sibling = sibling_of(here, 0)
    cube, inflow = join_stage(0, here, sibling)
    own = call(group_moments, [VMEM], [(4 * PART, LANES)], 300, after=[cube])(near)
    other = lax.ppermute(own, "px", [(i, i ^ GROUP) for i in range(px)])
    pair_chunk = (groups // 2, 4 * PART, LANES)
    far = call(
        functools.partial(pair_moments, ring),
        [VMEM] * 2,
        [pair_chunk],
        300,
        staged(pair_chunk[1:], groups // 2),
        to=ANY,
    )(own, other)
    far = lax.all_to_all(far, "px", 0, 0, tiled=True, axis_index_groups=across)

    for stage in range(1, stages):
        sibling = sibling_of(cube, stage)
        if stage < stages - 1:
            cube, inflow = join_stage(stage, cube, sibling, inflow)
    from_below = lax.ppermute(high, "px", [(i, (i + 1) % px) for i in range(px)])
    from_above = lax.ppermute(low, "px", [((i + 1) % px, i) for i in range(px)])

    back = call(
        functools.partial(entering, ring),
        [VMEM] * 3,
        [chunk],
        400,
        staged(chunk, GROUP),
        after=[from_below, from_above],
        to=ANY,
    )(near, other, far)
    acc, u = call(
        functools.partial(local_terms, stages - 1),
        [SMEM] * 4 + [VMEM] * 6,
        [(ROWS * XB, LANES), (YB * XB, LANES)],
        5000,
        [pltpu.VMEM((2, ROWS * XB, LANES), jnp.float32), pltpu.VMEM((ROWS * XB, LANES), jnp.float32)],
        after=[back],
    )(place, wall, metric_first, metric_second, v, from_below, from_above, cube, sibling, inflow)
    back = lax.all_to_all(back, "px", 0, 0, tiled=True, axis_index_groups=adjacent)
    out = call(finish, [VMEM] * 3, [whole], 800, staged(whole, GROUP), to=ANY)(acc, u, back)
    return out.reshape(velocity.shape)


def solution(mesh):
    return jax.shard_map(
        on_device,
        mesh=mesh,
        in_specs=(P(None, "pz", "px", None), P(), P()),
        out_specs=P(None, "pz", "px", None),
        check_vma=False,
    )
```

profile of v0, /device:TPU:18, one launch (start us, length us, event | category | flops | bytes accessed | tf_op | source)
XLA Modules:
  0.0 76.8 jit_solution(1682679132026158042)
XLA Ops:
  0.0 0.0 copy-start
  0.0 2.1 %shard_map.49 = f32[8,96,128]{2,1,0:T(8,128)} custom-call(f32[1536,128]{1,0:T(8,128)} %bitcast.4), custom_call_target="tpu_custom_call" | custom-call | flops 1536000 | bytes 786432 | tf_op jit(solution)/shard_map/pallas_call | solution.py:421
  2.1 6.2 %all-to-all-start = ((f32[8,96,128]{2,1,0:T(8,128)}), f32[8,96,128]{2,1,0:T(8,128)S(1)}, u32[]{:S(2)}, u32[]{:S(2)}) async-start(f32[8,96,128]{2,1,0:T(8,128)} %shard_map.49), calls=%async_computation | async-start | bytes 786432 | tf_op jit(solution)/shard_map/all_to_all | solution.py:442
  8.3 0.0 copy-start.1
  8.3 0.1 pad_add_fusion.refs_0_
  8.4 0.0 copy-done
  8.4 0.6 copy-done.1
  9.0 0.9 %shard_map.46 = (f32[144,128]{1,0:T(8,128)S(1)}, f32[192,128]{1,0:T(8,128)S(1)}, f32[192,128]{1,0:T(8,128)S(1)}) custom-call(s32[2]{0:T(128)S(1)} %pad_add_fusion.refs_0_, f32[8,66]{1,0:T(8,128)S(1)} %copy-done.1, f32[1536,128]{1,0:T(8,128)S(1)} %bitcast.5), custom_call_target="tpu_custom_call" | custom-call | flops 1536000 | bytes 540672 | tf_op jit(solution)/shard_map/pallas_call | solution.py:421
  9.9 1.9 %collective-permute-start.2 = (f32[144,128]{1,0:T(8,128)S(1)}, f32[144,128]{1,0:T(8,128)S(1)}, u32[]{:S(2)}, u32[]{:S(2)}) collective-permute-start(f32[144,128]{1,0:T(8,128)S(1)} %get-tuple-element.16.refs_0_), channel_id=1, source_target_pairs={{0,1},{1,0},{2,3},{3,2},{4,5},{5,4},{6,7},{7,6},{8,9},{9,8},{10,11... | collective-permute-start | bytes 221192 | tf_op jit(solution)/shard_map/ppermute | solution.py:448
  11.8 1.2 %collective-permute-done.2.refs_1_ = f32[144,128]{1,0:T(8,128)S(1)} collective-permute-done((f32[144,128]{1,0:T(8,128)S(1)}, f32[144,128]{1,0:T(8,128)S(1)}, u32[]{:S(2)}, u32[]{:S(2)}) %collective-permute-start.2) | collective-permute-done | bytes 73760 | tf_op jit(solution)/shard_map/ppermute | solution.py:448
  13.1 1.8 %all-to-all-done.refs_0_ = f32[8,96,128]{2,1,0:T(8,128)S(1)} async-done(((f32[8,96,128]{2,1,0:T(8,128)}), f32[8,96,128]{2,1,0:T(8,128)S(1)}, u32[]{:S(2)}, u32[]{:S(2)}) %all-to-all-start) | async-done | bytes 393248 | tf_op jit(solution)/shard_map/all_to_all | solution.py:442
  14.9 5.2 %collective-permute-start.5 = (f32[96,128]{1,0:T(8,128)S(1)}, f32[96,128]{1,0:T(8,128)S(1)}, u32[]{:S(2)}, u32[]{:S(2)}) collective-permute-start(f32[96,128]{1,0:T(8,128)S(1)} %shard_map.50.refs_0_), channel_id=1, source_target_pairs={{0,64},{8,72},{16,80},{24,88},{32,96},{40,104},{48,112},{56,120},{... | collective-permute-start | bytes 147464 | tf_op jit(solution)/shard_map/ppermute | solution.py:459
  20.1 3.1 %collective-permute-done.5.refs_1_ = f32[96,128]{1,0:T(8,128)S(1)} collective-permute-done((f32[96,128]{1,0:T(8,128)S(1)}, f32[96,128]{1,0:T(8,128)S(1)}, u32[]{:S(2)}, u32[]{:S(2)}) %collective-permute-start.5) | collective-permute-done | bytes 49184 | tf_op jit(solution)/shard_map/ppermute | solution.py:459
  23.2 0.7 shard_map.51
  23.9 13.0 %all-to-all-start.1 = ((f32[4,96,128]{2,1,0:T(8,128)}), f32[4,96,128]{2,1,0:T(8,128)S(1)}, u32[]{:S(2)}, u32[]{:S(2)}) async-start(f32[4,96,128]{2,1,0:T(8,128)} %shard_map.51), calls=%async_computation.1 | async-start | bytes 393216 | tf_op jit(solution)/shard_map/all_to_all | solution.py:469
  37.0 3.1 %collective-permute-start = (f32[192,128]{1,0:T(8,128)S(1)}, f32[192,128]{1,0:T(8,128)S(1)}, u32[]{:S(2)}, u32[]{:S(2)}) collective-permute-start(f32[192,128]{1,0:T(8,128)S(1)} %get-tuple-element.14), channel_id=1, source_target_pairs={{0,8},{8,16},{16,24},{24,32},{32,40},{40,48},{48,56},{56,64},{64,7... | collective-permute-start | bytes 294920 | tf_op jit(solution)/shard_map/ppermute | solution.py:475
  40.0 2.9 %collective-permute-start.1 = (f32[192,128]{1,0:T(8,128)S(1)}, f32[192,128]{1,0:T(8,128)S(1)}, u32[]{:S(2)}, u32[]{:S(2)}) collective-permute-start(f32[192,128]{1,0:T(8,128)S(1)} %get-tuple-element.15), channel_id=1, source_target_pairs={{8,0},{16,8},{24,16},{32,24},{40,32},{48,40},{56,48},{64,56},{72,6... | collective-permute-start | bytes 294920 | tf_op jit(solution)/shard_map/ppermute | solution.py:476
  42.9 0.7 collective-permute-done.refs_3_.refs_5_
  43.6 3.0 %collective-permute-done.1.refs_4_.refs_6_ = f32[192,128]{1,0:T(8,128)S(1)} collective-permute-done((f32[192,128]{1,0:T(8,128)S(1)}, f32[192,128]{1,0:T(8,128)S(1)}, u32[]{:S(2)}, u32[]{:S(2)}) %collective-permute-start.1) | collective-permute-done | bytes 98336 | tf_op jit(solution)/shard_map/ppermute | solution.py:476
  46.6 6.1 %all-to-all-done.1.refs_2_ = f32[4,96,128]{2,1,0:T(8,128)S(1)} async-done(((f32[4,96,128]{2,1,0:T(8,128)}), f32[4,96,128]{2,1,0:T(8,128)S(1)}, u32[]{:S(2)}, u32[]{:S(2)}) %all-to-all-start.1) | async-done | bytes 196640 | tf_op jit(solution)/shard_map/all_to_all | solution.py:469
  52.6 0.9 %shard_map.52.refs_10_ = f32[8,96,128]{2,1,0:T(8,128)} custom-call(f32[8,96,128]{2,1,0:T(8,128)S(1)} %all-to-all-done.refs_0_, f32[96,128]{1,0:T(8,128)S(1)} %collective-permute-done.5.refs_1_, f32[4,96,128]{2,1,0:T(8,128)S(1)} %all-to-all-done.1.refs_2_, f32[192,128]{1,0:T(8,128)S(1)} %collective-permute-done.refs_3_.refs_5_, ...), custom_call_target="tpu_custom_call" | custom-call | flops 409600 | bytes 786432 | tf_op jit(solution)/shard_map/pallas_call | solution.py:421
  53.5 5.7 %all-to-all-start.2 = ((f32[8,96,128]{2,1,0:T(8,128)}), f32[8,96,128]{2,1,0:T(8,128)S(1)}, u32[]{:S(2)}, u32[]{:S(2)}) async-start(f32[8,96,128]{2,1,0:T(8,128)} %shard_map.52.refs_10_), calls=%async_computation.2 | async-start | bytes 786432 | tf_op jit(solution)/shard_map/all_to_all | solution.py:495
  59.2 3.2 %collective-permute-start.3 = (f32[144,128]{1,0:T(8,128)S(1)}, f32[144,128]{1,0:T(8,128)S(1)}, u32[]{:S(2)}, u32[]{:S(2)}) collective-permute-start(f32[144,128]{1,0:T(8,128)S(1)} %get-tuple-element.17.refs_0_.refs_1_), channel_id=1, source_target_pairs={{0,2},{1,3},{2,0},{3,1},{4,6},{5,7},{6,4},{7,5},{8,10},{9,11},{10,... | collective-permute-start | bytes 221192 | tf_op jit(solution)/shard_map/ppermute | solution.py:448
  62.4 3.3 %collective-permute-done.3.refs_1_ = f32[144,128]{1,0:T(8,128)S(1)} collective-permute-done((f32[144,128]{1,0:T(8,128)S(1)}, f32[144,128]{1,0:T(8,128)S(1)}, u32[]{:S(2)}, u32[]{:S(2)}) %collective-permute-start.3) | collective-permute-done | bytes 73760 | tf_op jit(solution)/shard_map/ppermute | solution.py:448
  65.7 0.0 copy-start.3
  65.7 0.0 copy-start.2
  65.8 2.0 %collective-permute-start.4 = (f32[144,128]{1,0:T(8,128)S(1)}, f32[144,128]{1,0:T(8,128)S(1)}, u32[]{:S(2)}, u32[]{:S(2)}) collective-permute-start(f32[144,128]{1,0:T(8,128)S(1)} %get-tuple-element.19.refs_7_), channel_id=1, source_target_pairs={{0,4},{1,5},{2,6},{3,7},{4,0},{5,1},{6,2},{7,3},{8,12},{9,13},{10,... | collective-permute-start | bytes 221192 | tf_op jit(solution)/shard_map/ppermute | solution.py:448
  67.7 5.8 %collective-permute-done.4.refs_8_ = f32[144,128]{1,0:T(8,128)S(1)} collective-permute-done((f32[144,128]{1,0:T(8,128)S(1)}, f32[144,128]{1,0:T(8,128)S(1)}, u32[]{:S(2)}, u32[]{:S(2)}) %collective-permute-start.4) | collective-permute-done | bytes 73760 | tf_op jit(solution)/shard_map/ppermute | solution.py:448
  73.5 0.0 copy-done.3
  73.5 0.0 copy-done.2
  73.5 2.3 %shard_map.53 = (f32[1536,128]{1,0:T(8,128)S(1)}, f32[512,128]{1,0:T(8,128)S(1)}) custom-call(s32[2]{0:T(128)S(1)} %pad_add_fusion.refs_0_, f32[8,66]{1,0:T(8,128)S(1)} %copy-done.1, f32[512]{0:T(512)S(1)} %copy-done.2, f32[512]{0:T(512)S(1)} %copy-done.3, f32[1536,128]{1,0:T(8,128)S(1)} %bitcast.6, f32[192,128]{1,0:T(8,128)S(1)} %collective-permute-done.refs_3_.refs_5_, ...), custom_call_target="tpu_custom_call" | custom-call | flops 5120000 | bytes 2097152 | tf_op jit(solution)/shard_map/pallas_call | solution.py:421
  75.8 0.0 all-to-all-done.2.refs_2_
  75.8 1.0 %shard_map.54 = f32[1536,128]{1,0:T(8,128)} custom-call(f32[1536,128]{1,0:T(8,128)S(1)} %get-tuple-element.21.refs_0_, f32[512,128]{1,0:T(8,128)S(1)} %get-tuple-element.22.refs_1_, f32[8,96,128]{2,1,0:T(8,128)S(1)} %all-to-all-done.2.refs_2_), custom_call_target="tpu_custom_call" | custom-call | flops 819200 | bytes 1572864 | tf_op jit(solution)/shard_map/pallas_call | solution.py:421
  (3 shorter events, 0.1 us)
Async XLA Ops:
  0.0 8.4 %copy-start = (f32[3,64,8,128]{3,2,1,0:T(8,128)S(1)}, f32[3,64,8,128]{3,2,1,0:T(8,128)}, u32[]{:S(2)}) copy-start(f32[3,64,8,128]{3,2,1,0:T(8,128)} %param.4) | copy-start | bytes 2359300
  2.1 12.8 %all-to-all-start = ((f32[8,96,128]{2,1,0:T(8,128)}), f32[8,96,128]{2,1,0:T(8,128)S(1)}, u32[]{:S(2)}, u32[]{:S(2)}) async-start(f32[8,96,128]{2,1,0:T(8,128)} %shard_map.49), calls=%async_computation | async-start | bytes 786432 | tf_op jit(solution)/shard_map/all_to_all | solution.py:442
  8.3 0.7 copy-start.1
  9.9 3.2 %collective-permute-start.2 = (f32[144,128]{1,0:T(8,128)S(1)}, f32[144,128]{1,0:T(8,128)S(1)}, u32[]{:S(2)}, u32[]{:S(2)}) collective-permute-start(f32[144,128]{1,0:T(8,128)S(1)} %get-tuple-element.16.refs_0_), channel_id=1, source_target_pairs={{0,1},{1,0},{2,3},{3,2},{4,5},{5,4},{6,7},{7,6},{8,9},{9,8},{10,11... | collective-permute-start | bytes 221192 | tf_op jit(solution)/shard_map/ppermute | solution.py:448
  14.9 8.3 %collective-permute-start.5 = (f32[96,128]{1,0:T(8,128)S(1)}, f32[96,128]{1,0:T(8,128)S(1)}, u32[]{:S(2)}, u32[]{:S(2)}) collective-permute-start(f32[96,128]{1,0:T(8,128)S(1)} %shard_map.50.refs_0_), channel_id=1, source_target_pairs={{0,64},{8,72},{16,80},{24,88},{32,96},{40,104},{48,112},{56,120},{... | collective-permute-start | bytes 147464 | tf_op jit(solution)/shard_map/ppermute | solution.py:459
  23.9 28.7 %all-to-all-start.1 = ((f32[4,96,128]{2,1,0:T(8,128)}), f32[4,96,128]{2,1,0:T(8,128)S(1)}, u32[]{:S(2)}, u32[]{:S(2)}) async-start(f32[4,96,128]{2,1,0:T(8,128)} %shard_map.51), calls=%async_computation.1 | async-start | bytes 393216 | tf_op jit(solution)/shard_map/all_to_all | solution.py:469
  37.0 6.6 %collective-permute-start = (f32[192,128]{1,0:T(8,128)S(1)}, f32[192,128]{1,0:T(8,128)S(1)}, u32[]{:S(2)}, u32[]{:S(2)}) collective-permute-start(f32[192,128]{1,0:T(8,128)S(1)} %get-tuple-element.14), channel_id=1, source_target_pairs={{0,8},{8,16},{16,24},{24,32},{32,40},{40,48},{48,56},{56,64},{64,7... | collective-permute-start | bytes 294920 | tf_op jit(solution)/shard_map/ppermute | solution.py:475
  40.0 6.5 %collective-permute-start.1 = (f32[192,128]{1,0:T(8,128)S(1)}, f32[192,128]{1,0:T(8,128)S(1)}, u32[]{:S(2)}, u32[]{:S(2)}) collective-permute-start(f32[192,128]{1,0:T(8,128)S(1)} %get-tuple-element.15), channel_id=1, source_target_pairs={{8,0},{16,8},{24,16},{32,24},{40,32},{48,40},{56,48},{64,56},{72,6... | collective-permute-start | bytes 294920 | tf_op jit(solution)/shard_map/ppermute | solution.py:476
  53.5 22.3 %all-to-all-start.2 = ((f32[8,96,128]{2,1,0:T(8,128)}), f32[8,96,128]{2,1,0:T(8,128)S(1)}, u32[]{:S(2)}, u32[]{:S(2)}) async-start(f32[8,96,128]{2,1,0:T(8,128)} %shard_map.52.refs_10_), calls=%async_computation.2 | async-start | bytes 786432 | tf_op jit(solution)/shard_map/all_to_all | solution.py:495
  59.2 6.5 %collective-permute-start.3 = (f32[144,128]{1,0:T(8,128)S(1)}, f32[144,128]{1,0:T(8,128)S(1)}, u32[]{:S(2)}, u32[]{:S(2)}) collective-permute-start(f32[144,128]{1,0:T(8,128)S(1)} %get-tuple-element.17.refs_0_.refs_1_), channel_id=1, source_target_pairs={{0,2},{1,3},{2,0},{3,1},{4,6},{5,7},{6,4},{7,5},{8,10},{9,11},{10,... | collective-permute-start | bytes 221192 | tf_op jit(solution)/shard_map/ppermute | solution.py:448
  65.7 7.8 %copy-start.3 = (f32[512]{0:T(512)S(1)}, f32[512]{0:T(512)}, u32[]{:S(2)}) copy-start(f32[512]{0:T(512)} %refs_3_.1) | copy-start | bytes 6148
  65.7 7.8 %copy-start.2 = (f32[512]{0:T(512)S(1)}, f32[512]{0:T(512)}, u32[]{:S(2)}) copy-start(f32[512]{0:T(512)} %refs_2_.1) | copy-start | bytes 6148
  65.8 7.8 %collective-permute-start.4 = (f32[144,128]{1,0:T(8,128)S(1)}, f32[144,128]{1,0:T(8,128)S(1)}, u32[]{:S(2)}, u32[]{:S(2)}) collective-permute-start(f32[144,128]{1,0:T(8,128)S(1)} %get-tuple-element.19.refs_7_), channel_id=1, source_target_pairs={{0,4},{1,5},{2,6},{3,7},{4,0},{5,1},{6,2},{7,3},{8,12},{9,13},{10,... | collective-permute-start | bytes 221192 | tf_op jit(solution)/shard_map/ppermute | solution.py:448
where the time goes:
time: 77.4 us; the launch traced here: 76.8 us
  starting transfers between devices  43.2 us (56%)
  waiting for transfers between devices  24.9 us (32%)
  Pallas kernels  7.98 us (10%)
    all_to_all x1, starting transfers between devices, on_device(): far = lax.all_to_all(far, 'px', 0, 0, tiled=True, axis_index_groups=across)  13 us
    ppermute x3, waiting for transfers between devices, sibling_of(): return lax.ppermute(cube, 'pz', [(i, i ^ 1 << stage) for i in range(pz)])  10.3 us
    pallas_call x9, Pallas kernels, run(): return kernel(*arrays, *after)  7.98 us
    ppermute x3, starting transfers between devices, sibling_of(): return lax.ppermute(cube, 'pz', [(i, i ^ 1 << stage) for i in range(pz)])  7.08 us
    all_to_all x1, starting transfers between devices, on_device(): lax.all_to_all(near, 'px', 0, 0, tiled=True, axis_index_groups=adjacent)  6.2 us
    all_to_all x1, waiting for transfers between devices, on_device(): far = lax.all_to_all(far, 'px', 0, 0, tiled=True, axis_index_groups=across)  6.07 us
    all_to_all x1, starting transfers between devices, on_device(): lax.all_to_all(back, 'px', 0, 0, tiled=True, axis_index_groups=adjacent)  5.71 us
    ppermute x1, starting transfers between devices, on_device(): other = lax.ppermute(own, 'px', [(i, i ^ GROUP) for i in range(px)])  5.18 us
  transfers between devices with their start and end apart: 9, of which 8 were waited for; matrix products, arithmetic and copies ran while one was open for 0% of the time, Pallas kernels for 4%

commit v1 on v0

--- a/solution.py
+++ b/solution.py
@@ -476,13 +476,7 @@
     from_above = lax.ppermute(low, "px", [((i + 1) % px, i) for i in range(px)])
 
     back = call(
-        functools.partial(entering, ring),
-        [VMEM] * 3,
-        [chunk],
-        400,
-        staged(chunk, GROUP),
-        after=[from_below, from_above],
-        to=ANY,
+        functools.partial(entering, ring), [VMEM] * 3, [chunk], 400, staged(chunk, GROUP), to=ANY
     )(near, other, far)
     acc, u = call(
         functools.partial(local_terms, stages - 1),

time: 77.4 us -> 82.4 us (1.065)
  the two profiles are of different devices: /device:TPU:18 before, /device:TPU:16 now
where the time goes in v1:
time: 82.4 us; the launch traced here: 81.9 us
  starting transfers between devices  31.9 us (39%)
  blocking collectives  28.9 us (35%)
  waiting for transfers between devices  12.7 us (15%)
  Pallas kernels  7.58 us (9%)
    all_to_all x1, blocking collectives, on_device(): far = lax.all_to_all(far, 'px', 0, 0, tiled=True, axis_index_groups=across)  28.9 us
    ppermute x3, starting transfers between devices, sibling_of(): return lax.ppermute(cube, 'pz', [(i, i ^ 1 << stage) for i in range(pz)])  7.63 us
    pallas_call x9, Pallas kernels, run(): return kernel(*arrays, *after)  7.58 us
    ppermute x3, waiting for transfers between devices, sibling_of(): return lax.ppermute(cube, 'pz', [(i, i ^ 1 << stage) for i in range(pz)])  6.42 us
    all_to_all x1, starting transfers between devices, on_device(): lax.all_to_all(near, 'px', 0, 0, tiled=True, axis_index_groups=adjacent)  5.67 us
    ppermute x1, starting transfers between devices, on_device(): from_above = lax.ppermute(low, 'px', [((i + 1) % px, i) for i in range(px)])  5.23 us
    ppermute x1, starting transfers between devices, on_device(): other = lax.ppermute(own, 'px', [(i, i ^ GROUP) for i in range(px)])  5.18 us
    all_to_all x1, starting transfers between devices, on_device(): lax.all_to_all(back, 'px', 0, 0, tiled=True, axis_index_groups=adjacent)  4.24 us
  transfers between devices with their start and end apart: 8, of which 4 were waited for; matrix products, arithmetic and copies ran while one was open for 0% of the time, Pallas kernels for 4%

profile of v1, /device:TPU:16, one launch (start us, length us, event | category | flops | bytes accessed | tf_op | source)
XLA Modules:
  0.0 81.9 jit_solution(4546105137631718576)
XLA Ops:
  0.0 0.0 copy-start
  0.0 2.1 %shard_map.49 = f32[8,96,128]{2,1,0:T(8,128)} custom-call(f32[1536,128]{1,0:T(8,128)} %bitcast.4), custom_call_target="tpu_custom_call" | custom-call | flops 1536000 | bytes 786432 | tf_op jit(solution)/shard_map/pallas_call | solution.py:421
  2.1 5.7 %all-to-all-start = ((f32[8,96,128]{2,1,0:T(8,128)}), f32[8,96,128]{2,1,0:T(8,128)S(1)}, u32[]{:S(2)}, u32[]{:S(2)}) async-start(f32[8,96,128]{2,1,0:T(8,128)} %shard_map.49), calls=%async_computation | async-start | bytes 786432 | tf_op jit(solution)/shard_map/all_to_all | solution.py:442
  7.8 0.0 copy-start.1
  7.8 0.1 pad_add_fusion.refs_0_
  7.8 0.0 copy-done
  7.8 0.6 copy-done.1
  8.5 0.9 %shard_map.46 = (f32[144,128]{1,0:T(8,128)S(1)}, f32[192,128]{1,0:T(8,128)S(1)}, f32[192,128]{1,0:T(8,128)S(1)}) custom-call(s32[2]{0:T(128)S(1)} %pad_add_fusion.refs_0_, f32[8,66]{1,0:T(8,128)S(1)} %copy-done.1, f32[1536,128]{1,0:T(8,128)S(1)} %bitcast.5), custom_call_target="tpu_custom_call" | custom-call | flops 1536000 | bytes 540672 | tf_op jit(solution)/shard_map/pallas_call | solution.py:421
  9.3 1.9 %collective-permute-start.2 = (f32[144,128]{1,0:T(8,128)S(1)}, f32[144,128]{1,0:T(8,128)S(1)}, u32[]{:S(2)}, u32[]{:S(2)}) collective-permute-start(f32[144,128]{1,0:T(8,128)S(1)} %get-tuple-element.16.refs_0_), channel_id=1, source_target_pairs={{0,1},{1,0},{2,3},{3,2},{4,5},{5,4},{6,7},{7,6},{8,9},{9,8},{10,11... | collective-permute-start | bytes 221192 | tf_op jit(solution)/shard_map/ppermute | solution.py:448
  11.3 1.2 %collective-permute-done.2.refs_1_ = f32[144,128]{1,0:T(8,128)S(1)} collective-permute-done((f32[144,128]{1,0:T(8,128)S(1)}, f32[144,128]{1,0:T(8,128)S(1)}, u32[]{:S(2)}, u32[]{:S(2)}) %collective-permute-start.2) | collective-permute-done | bytes 73760 | tf_op jit(solution)/shard_map/ppermute | solution.py:448
  12.5 3.7 %all-to-all-done.refs_0_ = f32[8,96,128]{2,1,0:T(8,128)S(1)} async-done(((f32[8,96,128]{2,1,0:T(8,128)}), f32[8,96,128]{2,1,0:T(8,128)S(1)}, u32[]{:S(2)}, u32[]{:S(2)}) %all-to-all-start) | async-done | bytes 393248 | tf_op jit(solution)/shard_map/all_to_all | solution.py:442
  16.2 5.2 %collective-permute-start.5 = (f32[96,128]{1,0:T(8,128)S(1)}, f32[96,128]{1,0:T(8,128)S(1)}, u32[]{:S(2)}, u32[]{:S(2)}) collective-permute-start(f32[96,128]{1,0:T(8,128)S(1)} %shard_map.50.refs_0_), channel_id=1, source_target_pairs={{0,64},{8,72},{16,80},{24,88},{32,96},{40,104},{48,112},{56,120},{... | collective-permute-start | bytes 147464 | tf_op jit(solution)/shard_map/ppermute | solution.py:459
  21.4 2.6 %collective-permute-done.5.refs_1_ = f32[96,128]{1,0:T(8,128)S(1)} collective-permute-done((f32[96,128]{1,0:T(8,128)S(1)}, f32[96,128]{1,0:T(8,128)S(1)}, u32[]{:S(2)}, u32[]{:S(2)}) %collective-permute-start.5) | collective-permute-done | bytes 49184 | tf_op jit(solution)/shard_map/ppermute | solution.py:459
  24.0 0.3 shard_map.51
  24.3 28.9 %all_to_all.15.refs_2_ = f32[4,96,128]{2,1,0:T(8,128)S(1)} all-to-all(f32[4,96,128]{2,1,0:T(8,128)S(1)} %shard_map.51), channel_id=1, replica_groups={{0,128,256,384},{8,136,264,392},{16,144,272,400},{24,152,280,408},{32,1..., dimensions={0} | all-to-all | bytes 393216 | tf_op jit(solution)/shard_map/all_to_all | solution.py:469
  53.2 0.9 %shard_map.52.refs_10_ = f32[8,96,128]{2,1,0:T(8,128)} custom-call(f32[8,96,128]{2,1,0:T(8,128)S(1)} %all-to-all-done.refs_0_, f32[96,128]{1,0:T(8,128)S(1)} %collective-permute-done.5.refs_1_, f32[4,96,128]{2,1,0:T(8,128)S(1)} %all_to_all.15.refs_2_), custom_call_target="tpu_custom_call" | custom-call | flops 409600 | bytes 786432 | tf_op jit(solution)/shard_map/pallas_call | solution.py:421
  54.1 4.2 %all-to-all-start.2 = ((f32[8,96,128]{2,1,0:T(8,128)}), f32[8,96,128]{2,1,0:T(8,128)S(1)}, u32[]{:S(2)}, u32[]{:S(2)}) async-start(f32[8,96,128]{2,1,0:T(8,128)} %shard_map.52.refs_10_), calls=%async_computation.2 | async-start | bytes 786432 | tf_op jit(solution)/shard_map/all_to_all | solution.py:489
  58.3 3.2 %collective-permute-start.3 = (f32[144,128]{1,0:T(8,128)S(1)}, f32[144,128]{1,0:T(8,128)S(1)}, u32[]{:S(2)}, u32[]{:S(2)}) collective-permute-start(f32[144,128]{1,0:T(8,128)S(1)} %get-tuple-element.17.refs_0_.refs_1_), channel_id=1, source_target_pairs={{0,2},{1,3},{2,0},{3,1},{4,6},{5,7},{6,4},{7,5},{8,10},{9,11},{10,... | collective-permute-start | bytes 221192 | tf_op jit(solution)/shard_map/ppermute | solution.py:448
  61.5 3.9 %collective-permute-start = (f32[192,128]{1,0:T(8,128)S(1)}, f32[192,128]{1,0:T(8,128)S(1)}, u32[]{:S(2)}, u32[]{:S(2)}) collective-permute-start(f32[192,128]{1,0:T(8,128)S(1)} %get-tuple-element.14), channel_id=1, source_target_pairs={{0,8},{8,16},{16,24},{24,32},{32,40},{40,48},{48,56},{56,64},{64,7... | collective-permute-start | bytes 294920 | tf_op jit(solution)/shard_map/ppermute | solution.py:475
  65.5 5.2 %collective-permute-start.1 = (f32[192,128]{1,0:T(8,128)S(1)}, f32[192,128]{1,0:T(8,128)S(1)}, u32[]{:S(2)}, u32[]{:S(2)}) collective-permute-start(f32[192,128]{1,0:T(8,128)S(1)} %get-tuple-element.15), channel_id=1, source_target_pairs={{8,0},{16,8},{24,16},{32,24},{40,32},{48,40},{56,48},{64,56},{72,6... | collective-permute-start | bytes 294920 | tf_op jit(solution)/shard_map/ppermute | solution.py:476
  70.7 0.0 collective-permute-done.3.refs_1_
  70.7 0.0 copy-start.3
  70.8 0.0 copy-start.2
  70.8 2.5 %collective-permute-start.4 = (f32[144,128]{1,0:T(8,128)S(1)}, f32[144,128]{1,0:T(8,128)S(1)}, u32[]{:S(2)}, u32[]{:S(2)}) collective-permute-start(f32[144,128]{1,0:T(8,128)S(1)} %get-tuple-element.19.refs_7_), channel_id=1, source_target_pairs={{0,4},{1,5},{2,6},{3,7},{4,0},{5,1},{6,2},{7,3},{8,12},{9,13},{10,... | collective-permute-start | bytes 221192 | tf_op jit(solution)/shard_map/ppermute | solution.py:448
  73.3 0.0 collective-permute-done.refs_5_
  73.3 0.0 collective-permute-done.1.refs_6_
  73.3 5.2 %collective-permute-done.4.refs_8_ = f32[144,128]{1,0:T(8,128)S(1)} collective-permute-done((f32[144,128]{1,0:T(8,128)S(1)}, f32[144,128]{1,0:T(8,128)S(1)}, u32[]{:S(2)}, u32[]{:S(2)}) %collective-permute-start.4) | collective-permute-done | bytes 73760 | tf_op jit(solution)/shard_map/ppermute | solution.py:448
  78.5 0.0 copy-done.3
  78.5 0.0 copy-done.2
  78.5 2.3 %shard_map.53 = (f32[1536,128]{1,0:T(8,128)S(1)}, f32[512,128]{1,0:T(8,128)S(1)}) custom-call(s32[2]{0:T(128)S(1)} %pad_add_fusion.refs_0_, f32[8,66]{1,0:T(8,128)S(1)} %copy-done.1, f32[512]{0:T(512)S(1)} %copy-done.2, f32[512]{0:T(512)S(1)} %copy-done.3, f32[1536,128]{1,0:T(8,128)S(1)} %bitcast.6, f32[192,128]{1,0:T(8,128)S(1)} %collective-permute-done.refs_5_, ...), custom_call_target="tpu_custom_call" | custom-call | flops 5120000 | bytes 2097152 | tf_op jit(solution)/shard_map/pallas_call | solution.py:421
  80.8 0.0 all-to-all-done.2.refs_2_
  80.8 1.0 %shard_map.54 = f32[1536,128]{1,0:T(8,128)} custom-call(f32[1536,128]{1,0:T(8,128)S(1)} %get-tuple-element.21.refs_0_, f32[512,128]{1,0:T(8,128)S(1)} %get-tuple-element.22.refs_1_, f32[8,96,128]{2,1,0:T(8,128)S(1)} %all-to-all-done.2.refs_2_), custom_call_target="tpu_custom_call" | custom-call | flops 819200 | bytes 1572864 | tf_op jit(solution)/shard_map/pallas_call | solution.py:421
  (3 shorter events, 0.1 us)
Async XLA Ops:
  0.0 7.8 %copy-start = (f32[3,64,8,128]{3,2,1,0:T(8,128)S(1)}, f32[3,64,8,128]{3,2,1,0:T(8,128)}, u32[]{:S(2)}) copy-start(f32[3,64,8,128]{3,2,1,0:T(8,128)} %param.4) | copy-start | bytes 2359300
  2.1 14.1 %all-to-all-start = ((f32[8,96,128]{2,1,0:T(8,128)}), f32[8,96,128]{2,1,0:T(8,128)S(1)}, u32[]{:S(2)}, u32[]{:S(2)}) async-start(f32[8,96,128]{2,1,0:T(8,128)} %shard_map.49), calls=%async_computation | async-start | bytes 786432 | tf_op jit(solution)/shard_map/all_to_all | solution.py:442
  7.8 0.7 copy-start.1
  9.3 3.2 %collective-permute-start.2 = (f32[144,128]{1,0:T(8,128)S(1)}, f32[144,128]{1,0:T(8,128)S(1)}, u32[]{:S(2)}, u32[]{:S(2)}) collective-permute-start(f32[144,128]{1,0:T(8,128)S(1)} %get-tuple-element.16.refs_0_), channel_id=1, source_target_pairs={{0,1},{1,0},{2,3},{3,2},{4,5},{5,4},{6,7},{7,6},{8,9},{9,8},{10,11... | collective-permute-start | bytes 221192 | tf_op jit(solution)/shard_map/ppermute | solution.py:448
  16.2 7.8 %collective-permute-start.5 = (f32[96,128]{1,0:T(8,128)S(1)}, f32[96,128]{1,0:T(8,128)S(1)}, u32[]{:S(2)}, u32[]{:S(2)}) collective-permute-start(f32[96,128]{1,0:T(8,128)S(1)} %shard_map.50.refs_0_), channel_id=1, source_target_pairs={{0,64},{8,72},{16,80},{24,88},{32,96},{40,104},{48,112},{56,120},{... | collective-permute-start | bytes 147464 | tf_op jit(solution)/shard_map/ppermute | solution.py:459
  54.1 26.7 %all-to-all-start.2 = ((f32[8,96,128]{2,1,0:T(8,128)}), f32[8,96,128]{2,1,0:T(8,128)S(1)}, u32[]{:S(2)}, u32[]{:S(2)}) async-start(f32[8,96,128]{2,1,0:T(8,128)} %shard_map.52.refs_10_), calls=%async_computation.2 | async-start | bytes 786432 | tf_op jit(solution)/shard_map/all_to_all | solution.py:489
  58.3 12.4 %collective-permute-start.3 = (f32[144,128]{1,0:T(8,128)S(1)}, f32[144,128]{1,0:T(8,128)S(1)}, u32[]{:S(2)}, u32[]{:S(2)}) collective-permute-start(f32[144,128]{1,0:T(8,128)S(1)} %get-tuple-element.17.refs_0_.refs_1_), channel_id=1, source_target_pairs={{0,2},{1,3},{2,0},{3,1},{4,6},{5,7},{6,4},{7,5},{8,10},{9,11},{10,... | collective-permute-start | bytes 221192 | tf_op jit(solution)/shard_map/ppermute | solution.py:448
  61.5 11.8 %collective-permute-start = (f32[192,128]{1,0:T(8,128)S(1)}, f32[192,128]{1,0:T(8,128)S(1)}, u32[]{:S(2)}, u32[]{:S(2)}) collective-permute-start(f32[192,128]{1,0:T(8,128)S(1)} %get-tuple-element.14), channel_id=1, source_target_pairs={{0,8},{8,16},{16,24},{24,32},{32,40},{40,48},{48,56},{56,64},{64,7... | collective-permute-start | bytes 294920 | tf_op jit(solution)/shard_map/ppermute | solution.py:475
  65.5 7.9 %collective-permute-start.1 = (f32[192,128]{1,0:T(8,128)S(1)}, f32[192,128]{1,0:T(8,128)S(1)}, u32[]{:S(2)}, u32[]{:S(2)}) collective-permute-start(f32[192,128]{1,0:T(8,128)S(1)} %get-tuple-element.15), channel_id=1, source_target_pairs={{8,0},{16,8},{24,16},{32,24},{40,32},{48,40},{56,48},{64,56},{72,6... | collective-permute-start | bytes 294920 | tf_op jit(solution)/shard_map/ppermute | solution.py:476
  70.7 7.8 %copy-start.3 = (f32[512]{0:T(512)S(1)}, f32[512]{0:T(512)}, u32[]{:S(2)}) copy-start(f32[512]{0:T(512)} %refs_3_.1) | copy-start | bytes 6148
  70.8 7.8 %copy-start.2 = (f32[512]{0:T(512)S(1)}, f32[512]{0:T(512)}, u32[]{:S(2)}) copy-start(f32[512]{0:T(512)} %refs_2_.1) | copy-start | bytes 6148
  70.8 7.8 %collective-permute-start.4 = (f32[144,128]{1,0:T(8,128)S(1)}, f32[144,128]{1,0:T(8,128)S(1)}, u32[]{:S(2)}, u32[]{:S(2)}) collective-permute-start(f32[144,128]{1,0:T(8,128)S(1)} %get-tuple-element.19.refs_7_), channel_id=1, source_target_pairs={{0,4},{1,5},{2,6},{3,7},{4,0},{5,1},{6,2},{7,3},{8,12},{9,13},{10,... | collective-permute-start | bytes 221192 | tf_op jit(solution)/shard_map/ppermute | solution.py:448

commit v2 on v1

--- a/solution.py
+++ b/solution.py
@@ -138,18 +138,11 @@
     return jnp.where(top_half((rows, LANES)), one, two)
 
 
-def moments_x(v_hbm, out_hbm, v_ref, out_ref, in_sems, out_sems):
-    def fetch(part):
-        rows = pl.ds(part * PART * XB, PART * XB)
-        return pltpu.make_async_copy(v_hbm.at[rows], v_ref.at[rows], in_sems.at[part])
-
+def moments_x(v_ref, out_hbm, out_ref, out_sems):
     def send(part):
         return pltpu.make_async_copy(out_ref.at[part], out_hbm.at[part], out_sems.at[part])
 
     for part in range(GROUP):
-        fetch(part).start()
-    for part in range(GROUP):
-        fetch(part).wait()
         for g in range(part * PART // 8, (part + 1) * PART // 8):
             sums = [None] * 4
             for i in range(XB):
@@ -362,9 +355,12 @@
 
 
 def finish(acc_ref, u_ref, far_ref, out_hbm, out_ref, sems):
-    def send(part):
-        rows = pl.ds(part * PART * XB, PART * XB)
-        return pltpu.make_async_copy(out_ref.at[rows], out_hbm.at[rows], sems.at[part])
+    count = sems.shape[0]
+    groups = ROWS // 8 // count
+
+    def send(piece):
+        rows = pl.ds(piece * groups * 64, groups * 64)
+        return pltpu.make_async_copy(out_ref.at[rows], out_hbm.at[rows], sems.at[piece])
 
     for g in range(ROWS // 8):
         sums = []
@@ -384,10 +380,10 @@
             u = u_ref[64 * (g % 8) + 8 * i : 64 * (g % 8) + 8 * i + 8, :]
             acc = acc_ref[64 * g + 8 * i : 64 * g + 8 * i + 8, :]
             out_ref[plane(64 * g, i), :] = (acc + two) - u * one
-        if 8 * (g + 1) % PART == 0:
-            send(8 * g // PART).start()
-    for part in range(GROUP):
-        send(part).wait()
+        if (g + 1) % groups == 0:
+            send(g // groups).start()
+    for piece in range(count):
+        send(piece).wait()
 
 
 VMEM = pl.BlockSpec(memory_space=pltpu.VMEM)
@@ -437,8 +433,7 @@
     v = velocity.reshape(ROWS * XB, LANES)
 
     whole = (ROWS * XB, LANES)
-    scratch = [pltpu.VMEM(whole, jnp.float32)] + staged(chunk, GROUP, GROUP)
-    near = call(moments_x, [ANY], [chunk], 1500, scratch, to=ANY, vmem=60)(v)
+    near = call(moments_x, [VMEM], [chunk], 1500, staged(chunk, GROUP), to=ANY)(v)
     near = lax.all_to_all(near, "px", 0, 0, tiled=True, axis_index_groups=adjacent)
     here, low, high = call(
         moments_y, [SMEM, SMEM, VMEM], [(6 * YROWS, LANES)] + [(ROWS, LANES)] * 2, 1500
@@ -487,7 +482,7 @@
         after=[back],
     )(place, wall, metric_first, metric_second, v, from_below, from_above, cube, sibling, inflow)
     back = lax.all_to_all(back, "px", 0, 0, tiled=True, axis_index_groups=adjacent)
-    out = call(finish, [VMEM] * 3, [whole], 800, staged(whole, GROUP), to=ANY)(acc, u, back)
+    out = call(finish, [VMEM] * 3, [whole], 800, staged(whole, 12), to=ANY)(acc, u, back)
     return out.reshape(velocity.shape)
 
 

time: 82.4 us -> 82.4 us (level)
  local copies, waits for them, and re-layouts: 0.62 us -> 1.75 us
  Pallas kernels: 7.58 us -> 6.47 us
    unnamed x8 -> x10, local copies, waits for them, and re-layouts: 0.62 us -> 1.75 us
    pallas_call x9, Pallas kernels: 7.58 us -> 6.47 us  [run(): return kernel(*arrays, *after)]
where the time goes in v2:
time: 82.4 us; the launch traced here: 81.9 us
  starting transfers between devices  31.9 us (39%)
  blocking collectives  28.9 us (35%)
  waiting for transfers between devices  12.7 us (15%)
  Pallas kernels  6.47 us (8%)
  local copies, waits for them, and re-layouts  1.75 us (2%)
    all_to_all x1, blocking collectives, on_device(): far = lax.all_to_all(far, 'px', 0, 0, tiled=True, axis_index_groups=across)  28.9 us
    ppermute x3, starting transfers between devices, sibling_of(): return lax.ppermute(cube, 'pz', [(i, i ^ 1 << stage) for i in range(pz)])  7.63 us
    pallas_call x9, Pallas kernels, run(): return kernel(*arrays, *after)  6.47 us
    ppermute x3, waiting for transfers between devices, sibling_of(): return lax.ppermute(cube, 'pz', [(i, i ^ 1 << stage) for i in range(pz)])  6.42 us
    all_to_all x1, starting transfers between devices, on_device(): lax.all_to_all(near, 'px', 0, 0, tiled=True, axis_index_groups=adjacent)  5.67 us
    ppermute x1, starting transfers between devices, on_device(): from_above = lax.ppermute(low, 'px', [((i + 1) % px, i) for i in range(px)])  5.23 us
    ppermute x1, starting transfers between devices, on_device(): other = lax.ppermute(own, 'px', [(i, i ^ GROUP) for i in range(px)])  5.18 us
    all_to_all x1, starting transfers between devices, on_device(): lax.all_to_all(back, 'px', 0, 0, tiled=True, axis_index_groups=adjacent)  4.24 us
  transfers between devices with their start and end apart: 8, of which 4 were waited for; matrix products, arithmetic and copies ran while one was open for 0% of the time, Pallas kernels for 4%

profile of v2, /device:TPU:16, one launch (start us, length us, event | category | flops | bytes accessed | tf_op | source)
XLA Modules:
  0.0 81.9 jit_solution(1522559374955275787)
XLA Ops:
  0.0 0.0 copy-start
  0.0 1.1 %copy-done = f32[3,64,8,128]{3,2,1,0:T(8,128)S(1)} copy-done((f32[3,64,8,128]{3,2,1,0:T(8,128)S(1)}, f32[3,64,8,128]{3,2,1,0:T(8,128)}, u32[]{:S(2)}) %copy-start) | copy-done | bytes 786456
  1.1 0.0 copy-start.1
  1.1 1.0 %shard_map.49 = f32[8,96,128]{2,1,0:T(8,128)} custom-call(f32[1536,128]{1,0:T(8,128)S(1)} %bitcast.4), custom_call_target="tpu_custom_call" | custom-call | flops 1536000 | bytes 786432 | tf_op jit(solution)/shard_map/pallas_call | solution.py:417
  2.1 5.7 %all-to-all-start = ((f32[8,96,128]{2,1,0:T(8,128)}), f32[8,96,128]{2,1,0:T(8,128)S(1)}, u32[]{:S(2)}, u32[]{:S(2)}) async-start(f32[8,96,128]{2,1,0:T(8,128)} %shard_map.49), calls=%async_computation | async-start | bytes 786432 | tf_op jit(solution)/shard_map/all_to_all | solution.py:437
  7.8 0.0 copy-start.2
  7.8 0.1 pad_add_fusion.refs_0_
  7.9 0.0 copy-done.1
  7.9 0.6 copy-done.2
  8.5 0.9 %shard_map.46 = (f32[144,128]{1,0:T(8,128)S(1)}, f32[192,128]{1,0:T(8,128)S(1)}, f32[192,128]{1,0:T(8,128)S(1)}) custom-call(s32[2]{0:T(128)S(1)} %pad_add_fusion.refs_0_, f32[8,66]{1,0:T(8,128)S(1)} %copy-done.2, f32[1536,128]{1,0:T(8,128)S(1)} %bitcast.5), custom_call_target="tpu_custom_call" | custom-call | flops 1536000 | bytes 540672 | tf_op jit(solution)/shard_map/pallas_call | solution.py:417
  9.4 1.9 %collective-permute-start.2 = (f32[144,128]{1,0:T(8,128)S(1)}, f32[144,128]{1,0:T(8,128)S(1)}, u32[]{:S(2)}, u32[]{:S(2)}) collective-permute-start(f32[144,128]{1,0:T(8,128)S(1)} %get-tuple-element.16.refs_0_), channel_id=1, source_target_pairs={{0,1},{1,0},{2,3},{3,2},{4,5},{5,4},{6,7},{7,6},{8,9},{9,8},{10,11... | collective-permute-start | bytes 221192 | tf_op jit(solution)/shard_map/ppermute | solution.py:443
  11.3 1.2 %collective-permute-done.2.refs_1_ = f32[144,128]{1,0:T(8,128)S(1)} collective-permute-done((f32[144,128]{1,0:T(8,128)S(1)}, f32[144,128]{1,0:T(8,128)S(1)}, u32[]{:S(2)}, u32[]{:S(2)}) %collective-permute-start.2) | collective-permute-done | bytes 73760 | tf_op jit(solution)/shard_map/ppermute | solution.py:443
  12.5 3.7 %all-to-all-done.refs_0_ = f32[8,96,128]{2,1,0:T(8,128)S(1)} async-done(((f32[8,96,128]{2,1,0:T(8,128)}), f32[8,96,128]{2,1,0:T(8,128)S(1)}, u32[]{:S(2)}, u32[]{:S(2)}) %all-to-all-start) | async-done | bytes 393248 | tf_op jit(solution)/shard_map/all_to_all | solution.py:437
  16.3 5.2 %collective-permute-start.5 = (f32[96,128]{1,0:T(8,128)S(1)}, f32[96,128]{1,0:T(8,128)S(1)}, u32[]{:S(2)}, u32[]{:S(2)}) collective-permute-start(f32[96,128]{1,0:T(8,128)S(1)} %shard_map.50.refs_0_), channel_id=1, source_target_pairs={{0,64},{8,72},{16,80},{24,88},{32,96},{40,104},{48,112},{56,120},{... | collective-permute-start | bytes 147464 | tf_op jit(solution)/shard_map/ppermute | solution.py:454
  21.4 2.6 %collective-permute-done.5.refs_1_ = f32[96,128]{1,0:T(8,128)S(1)} collective-permute-done((f32[96,128]{1,0:T(8,128)S(1)}, f32[96,128]{1,0:T(8,128)S(1)}, u32[]{:S(2)}, u32[]{:S(2)}) %collective-permute-start.5) | collective-permute-done | bytes 49184 | tf_op jit(solution)/shard_map/ppermute | solution.py:454
  24.0 0.3 shard_map.51
  24.3 28.9 %all_to_all.15.refs_2_ = f32[4,96,128]{2,1,0:T(8,128)S(1)} all-to-all(f32[4,96,128]{2,1,0:T(8,128)S(1)} %shard_map.51), channel_id=1, replica_groups={{0,128,256,384},{8,136,264,392},{16,144,272,400},{24,152,280,408},{32,1..., dimensions={0} | all-to-all | bytes 393216 | tf_op jit(solution)/shard_map/all_to_all | solution.py:464
  53.2 0.9 %shard_map.52.refs_10_ = f32[8,96,128]{2,1,0:T(8,128)} custom-call(f32[8,96,128]{2,1,0:T(8,128)S(1)} %all-to-all-done.refs_0_, f32[96,128]{1,0:T(8,128)S(1)} %collective-permute-done.5.refs_1_, f32[4,96,128]{2,1,0:T(8,128)S(1)} %all_to_all.15.refs_2_), custom_call_target="tpu_custom_call" | custom-call | flops 409600 | bytes 786432 | tf_op jit(solution)/shard_map/pallas_call | solution.py:417
  54.1 4.2 %all-to-all-start.2 = ((f32[8,96,128]{2,1,0:T(8,128)}), f32[8,96,128]{2,1,0:T(8,128)S(1)}, u32[]{:S(2)}, u32[]{:S(2)}) async-start(f32[8,96,128]{2,1,0:T(8,128)} %shard_map.52.refs_10_), calls=%async_computation.2 | async-start | bytes 786432 | tf_op jit(solution)/shard_map/all_to_all | solution.py:484
  58.3 3.2 %collective-permute-start.3 = (f32[144,128]{1,0:T(8,128)S(1)}, f32[144,128]{1,0:T(8,128)S(1)}, u32[]{:S(2)}, u32[]{:S(2)}) collective-permute-start(f32[144,128]{1,0:T(8,128)S(1)} %get-tuple-element.17.refs_0_.refs_1_), channel_id=1, source_target_pairs={{0,2},{1,3},{2,0},{3,1},{4,6},{5,7},{6,4},{7,5},{8,10},{9,11},{10,... | collective-permute-start | bytes 221192 | tf_op jit(solution)/shard_map/ppermute | solution.py:443
  61.5 3.9 %collective-permute-start = (f32[192,128]{1,0:T(8,128)S(1)}, f32[192,128]{1,0:T(8,128)S(1)}, u32[]{:S(2)}, u32[]{:S(2)}) collective-permute-start(f32[192,128]{1,0:T(8,128)S(1)} %get-tuple-element.14), channel_id=1, source_target_pairs={{0,8},{8,16},{16,24},{24,32},{32,40},{40,48},{48,56},{56,64},{64,7... | collective-permute-start | bytes 294920 | tf_op jit(solution)/shard_map/ppermute | solution.py:470
  65.5 5.2 %collective-permute-start.1 = (f32[192,128]{1,0:T(8,128)S(1)}, f32[192,128]{1,0:T(8,128)S(1)}, u32[]{:S(2)}, u32[]{:S(2)}) collective-permute-start(f32[192,128]{1,0:T(8,128)S(1)} %get-tuple-element.15), channel_id=1, source_target_pairs={{8,0},{16,8},{24,16},{32,24},{40,32},{48,40},{56,48},{64,56},{72,6... | collective-permute-start | bytes 294920 | tf_op jit(solution)/shard_map/ppermute | solution.py:471
  70.7 0.0 collective-permute-done.3.refs_1_
  70.7 0.0 copy-start.4
  70.8 0.0 copy-start.3
  70.8 2.5 %collective-permute-start.4 = (f32[144,128]{1,0:T(8,128)S(1)}, f32[144,128]{1,0:T(8,128)S(1)}, u32[]{:S(2)}, u32[]{:S(2)}) collective-permute-start(f32[144,128]{1,0:T(8,128)S(1)} %get-tuple-element.19.refs_7_), channel_id=1, source_target_pairs={{0,4},{1,5},{2,6},{3,7},{4,0},{5,1},{6,2},{7,3},{8,12},{9,13},{10,... | collective-permute-start | bytes 221192 | tf_op jit(solution)/shard_map/ppermute | solution.py:443
  73.3 0.0 collective-permute-done.refs_5_
  73.3 0.0 collective-permute-done.1.refs_6_
  73.3 5.2 %collective-permute-done.4.refs_8_ = f32[144,128]{1,0:T(8,128)S(1)} collective-permute-done((f32[144,128]{1,0:T(8,128)S(1)}, f32[144,128]{1,0:T(8,128)S(1)}, u32[]{:S(2)}, u32[]{:S(2)}) %collective-permute-start.4) | collective-permute-done | bytes 73760 | tf_op jit(solution)/shard_map/ppermute | solution.py:443
  78.5 0.0 copy-done.4
  78.5 0.0 copy-done.3
  78.5 2.3 %shard_map.53 = (f32[1536,128]{1,0:T(8,128)S(1)}, f32[512,128]{1,0:T(8,128)S(1)}) custom-call(s32[2]{0:T(128)S(1)} %pad_add_fusion.refs_0_, f32[8,66]{1,0:T(8,128)S(1)} %copy-done.2, f32[512]{0:T(512)S(1)} %copy-done.3, f32[512]{0:T(512)S(1)} %copy-done.4, f32[1536,128]{1,0:T(8,128)S(1)} %bitcast.6, f32[192,128]{1,0:T(8,128)S(1)} %collective-permute-done.refs_5_, ...), custom_call_target="tpu_custom_call" | custom-call | flops 5120000 | bytes 2097152 | tf_op jit(solution)/shard_map/pallas_call | solution.py:417
  80.8 0.0 all-to-all-done.2.refs_2_
  80.8 1.0 %shard_map.54 = f32[1536,128]{1,0:T(8,128)} custom-call(f32[1536,128]{1,0:T(8,128)S(1)} %get-tuple-element.21.refs_0_, f32[512,128]{1,0:T(8,128)S(1)} %get-tuple-element.22.refs_1_, f32[8,96,128]{2,1,0:T(8,128)S(1)} %all-to-all-done.2.refs_2_), custom_call_target="tpu_custom_call" | custom-call | flops 819200 | bytes 1572864 | tf_op jit(solution)/shard_map/pallas_call | solution.py:417
  (3 shorter events, 0.1 us)
Async XLA Ops:
  0.0 1.1 %copy-start = (f32[3,64,8,128]{3,2,1,0:T(8,128)S(1)}, f32[3,64,8,128]{3,2,1,0:T(8,128)}, u32[]{:S(2)}) copy-start(f32[3,64,8,128]{3,2,1,0:T(8,128)} %param.4) | copy-start | bytes 2359300
  1.1 6.7 %copy-start.1 = (f32[3,64,8,128]{3,2,1,0:T(8,128)S(1)}, f32[3,64,8,128]{3,2,1,0:T(8,128)}, u32[]{:S(2)}) copy-start(f32[3,64,8,128]{3,2,1,0:T(8,128)} %param.4) | copy-start | bytes 2359300
  2.1 14.1 %all-to-all-start = ((f32[8,96,128]{2,1,0:T(8,128)}), f32[8,96,128]{2,1,0:T(8,128)S(1)}, u32[]{:S(2)}, u32[]{:S(2)}) async-start(f32[8,96,128]{2,1,0:T(8,128)} %shard_map.49), calls=%async_computation | async-start | bytes 786432 | tf_op jit(solution)/shard_map/all_to_all | solution.py:437
  7.8 0.7 copy-start.2
  9.4 3.2 %collective-permute-start.2 = (f32[144,128]{1,0:T(8,128)S(1)}, f32[144,128]{1,0:T(8,128)S(1)}, u32[]{:S(2)}, u32[]{:S(2)}) collective-permute-start(f32[144,128]{1,0:T(8,128)S(1)} %get-tuple-element.16.refs_0_), channel_id=1, source_target_pairs={{0,1},{1,0},{2,3},{3,2},{4,5},{5,4},{6,7},{7,6},{8,9},{9,8},{10,11... | collective-permute-start | bytes 221192 | tf_op jit(solution)/shard_map/ppermute | solution.py:443
  16.3 7.8 %collective-permute-start.5 = (f32[96,128]{1,0:T(8,128)S(1)}, f32[96,128]{1,0:T(8,128)S(1)}, u32[]{:S(2)}, u32[]{:S(2)}) collective-permute-start(f32[96,128]{1,0:T(8,128)S(1)} %shard_map.50.refs_0_), channel_id=1, source_target_pairs={{0,64},{8,72},{16,80},{24,88},{32,96},{40,104},{48,112},{56,120},{... | collective-permute-start | bytes 147464 | tf_op jit(solution)/shard_map/ppermute | solution.py:454
  54.1 26.7 %all-to-all-start.2 = ((f32[8,96,128]{2,1,0:T(8,128)}), f32[8,96,128]{2,1,0:T(8,128)S(1)}, u32[]{:S(2)}, u32[]{:S(2)}) async-start(f32[8,96,128]{2,1,0:T(8,128)} %shard_map.52.refs_10_), calls=%async_computation.2 | async-start | bytes 786432 | tf_op jit(solution)/shard_map/all_to_all | solution.py:484
  58.3 12.4 %collective-permute-start.3 = (f32[144,128]{1,0:T(8,128)S(1)}, f32[144,128]{1,0:T(8,128)S(1)}, u32[]{:S(2)}, u32[]{:S(2)}) collective-permute-start(f32[144,128]{1,0:T(8,128)S(1)} %get-tuple-element.17.refs_0_.refs_1_), channel_id=1, source_target_pairs={{0,2},{1,3},{2,0},{3,1},{4,6},{5,7},{6,4},{7,5},{8,10},{9,11},{10,... | collective-permute-start | bytes 221192 | tf_op jit(solution)/shard_map/ppermute | solution.py:443
  61.5 11.8 %collective-permute-start = (f32[192,128]{1,0:T(8,128)S(1)}, f32[192,128]{1,0:T(8,128)S(1)}, u32[]{:S(2)}, u32[]{:S(2)}) collective-permute-start(f32[192,128]{1,0:T(8,128)S(1)} %get-tuple-element.14), channel_id=1, source_target_pairs={{0,8},{8,16},{16,24},{24,32},{32,40},{40,48},{48,56},{56,64},{64,7... | collective-permute-start | bytes 294920 | tf_op jit(solution)/shard_map/ppermute | solution.py:470
  65.5 7.9 %collective-permute-start.1 = (f32[192,128]{1,0:T(8,128)S(1)}, f32[192,128]{1,0:T(8,128)S(1)}, u32[]{:S(2)}, u32[]{:S(2)}) collective-permute-start(f32[192,128]{1,0:T(8,128)S(1)} %get-tuple-element.15), channel_id=1, source_target_pairs={{8,0},{16,8},{24,16},{32,24},{40,32},{48,40},{56,48},{64,56},{72,6... | collective-permute-start | bytes 294920 | tf_op jit(solution)/shard_map/ppermute | solution.py:471
  70.7 7.8 %copy-start.4 = (f32[512]{0:T(512)S(1)}, f32[512]{0:T(512)}, u32[]{:S(2)}) copy-start(f32[512]{0:T(512)} %refs_3_.1) | copy-start | bytes 6148
  70.8 7.8 %copy-start.3 = (f32[512]{0:T(512)S(1)}, f32[512]{0:T(512)}, u32[]{:S(2)}) copy-start(f32[512]{0:T(512)} %refs_2_.1) | copy-start | bytes 6148
  70.8 7.8 %collective-permute-start.4 = (f32[144,128]{1,0:T(8,128)S(1)}, f32[144,128]{1,0:T(8,128)S(1)}, u32[]{:S(2)}, u32[]{:S(2)}) collective-permute-start(f32[144,128]{1,0:T(8,128)S(1)} %get-tuple-element.19.refs_7_), channel_id=1, source_target_pairs={{0,4},{1,5},{2,6},{3,7},{4,0},{5,1},{6,2},{7,3},{8,12},{9,13},{10,... | collective-permute-start | bytes 221192 | tf_op jit(solution)/shard_map/ppermute | solution.py:443
